TPU v7x, 32 devices: a whole 2x2x4 slice. The times are simulated.
32 devices in a mesh: frame: 16 (over z, y, core), row: 2 (over x).
Axes of the slice: x: 2, y: 2, z: 4, core: 2. Of those that a mesh axis runs over, the one named last changes fastest.
Arguments:
- spatial_q: bfloat16 [16, 256, 3072], P('frame', 'row'), may hold values from -6 to 6
- spatial_k: bfloat16 [16, 256, 3072], P('frame', 'row'), may hold values from -6 to 6
- spatial_v: bfloat16 [16, 256, 3072], P('frame', 'row'), may hold values from -6 to 6
- norm_gain: float32 [3072], replicated, may hold values from 0.5 to 1.5
- temporal_weight: bfloat16 [3072, 3, 3072], P(None, None, 'row'), may hold values from -0.625 to 0.625
Outputs:
- temporal_out: bfloat16 [16, 256, 3072], P('frame', 'row')
All inputs are finite; a program needn't handle non-finite values.
Results may differ from a plain program's by a relative error of at most 0.0083.
Values may be sent and summed in bfloat16 or wider, within the bound.
No kernel may reach another device: no remote copies, remote signals or barrier semaphores. Data moves between devices by JAX's collectives and lax.ppermute only.
A program may use at most 64 MiB of HBM per device.

v0:
```python
import jax
import jax.numpy as jnp
from jax import lax
from jax.sharding import PartitionSpec as P

D = 3072
HEADS = 24
AGENTS = 128
epsilon = 1e-06


def local(spatial_q, spatial_k, spatial_v, norm_gain, temporal_weight):
    frame_count = lax.axis_size("frame")
    row_count = lax.axis_size("row")
    local_frames, local_tokens, width = spatial_q.shape
    head_size = D // HEADS
    scale = head_size ** (-0.5)
    pool_size = local_tokens * row_count // AGENTS
    own_agents = local_tokens // pool_size
    pooled = jnp.mean(
        spatial_q.reshape(local_frames, own_agents, pool_size, width), axis=2, dtype=jnp.float32
    )
    agents = lax.all_gather(pooled.astype(jnp.bfloat16), "row", axis=1, tiled=True)
    agent_heads = agents.reshape(local_frames, AGENTS, HEADS, head_size)
    query_heads = spatial_q.reshape(local_frames, local_tokens, HEADS, head_size)
    key_heads = spatial_k.reshape(local_frames, local_tokens, HEADS, head_size)
    value_heads = spatial_v.reshape(local_frames, local_tokens, HEADS, head_size)
    agent_scores = (
        jnp.einsum("fahd,fthd->fhat", agent_heads, key_heads, preferred_element_type=jnp.float32)
        * scale
    )
    peak = lax.pmax(jnp.max(agent_scores, axis=-1), "row")
    agent_weights = jnp.exp(agent_scores - peak[..., None])
    agent_totals = jnp.sum(agent_weights, axis=-1)
    agent_numer = jnp.einsum(
        "fhat,fthd->fhad",
        agent_weights.astype(jnp.bfloat16),
        value_heads,
        preferred_element_type=jnp.float32,
    )
    agent_totals, agent_numer = lax.psum((agent_totals, agent_numer), "row")
    agent_values = (agent_numer / agent_totals[..., None]).astype(jnp.bfloat16)
    token_scores = (
        jnp.einsum("fthd,fahd->fhta", query_heads, agent_heads, preferred_element_type=jnp.float32)
        * scale
    )
    token_weights = jax.nn.softmax(token_scores, axis=-1).astype(jnp.bfloat16)
    spatial_out = jnp.einsum(
        "fhta,fhad->fthd", token_weights, agent_values, preferred_element_type=jnp.float32
    )
    spatial_out = spatial_out.reshape(local_frames, local_tokens, width)
    mean_square = jnp.mean(spatial_out * spatial_out, axis=-1, keepdims=True)
    normed = (spatial_out * lax.rsqrt(mean_square + epsilon) * norm_gain).astype(jnp.bfloat16)
    slot_size = local_tokens // frame_count
    group_width = temporal_weight.shape[2]
    group_heads = group_width // head_size
    all_frames = local_frames * frame_count
    locations = row_count * slot_size
    packed = normed.reshape(local_frames, frame_count, slot_size, width)
    moved = lax.all_to_all(packed, "frame", split_axis=1, concat_axis=0, tiled=True)
    moved = moved.reshape(all_frames, slot_size, width)
    projected = jnp.einsum(
        "ftd,dcn->ftcn",
        lax.all_gather(moved, "row", axis=1, tiled=True),
        temporal_weight,
        preferred_element_type=jnp.float32,
    )
    qkv = projected.astype(jnp.bfloat16).reshape(all_frames, locations, 3, group_heads, head_size)
    temporal_scores = (
        jnp.einsum(
            "flhd,glhd->lhfg", qkv[:, :, 0], qkv[:, :, 1], preferred_element_type=jnp.float32
        )
        * scale
    )
    temporal_weights = jax.nn.softmax(temporal_scores, axis=-1).astype(jnp.bfloat16)
    attended = jnp.einsum(
        "lhfg,glhd->flhd", temporal_weights, qkv[:, :, 2], preferred_element_type=jnp.float32
    )
    attended = attended.astype(jnp.bfloat16).reshape(
        all_frames, row_count, 1, slot_size, group_width
    )
    gathered_heads = lax.all_to_all(attended, "row", split_axis=1, concat_axis=4, tiled=True)
    returned = lax.all_to_all(gathered_heads, "frame", split_axis=0, concat_axis=2, tiled=True)
    return returned.reshape(local_frames, local_tokens, width)


def solution(mesh):
    return jax.shard_map(
        local,
        mesh=mesh,
        in_specs=(
            P("frame", "row", None),
            P("frame", "row", None),
            P("frame", "row", None),
            P(),
            P(None, None, "row"),
        ),
        out_specs=P("frame", "row", None),
        check_vma=False,
    )
```

profile of v0, /device:TPU:1, one launch (start us, length us, event | category | flops | bytes accessed | tf_op | source)
XLA Modules:
  0.0 225.7 jit_solution(15268183589663754578)
XLA Ops:
  6.5 0.0 copy-start.3
  6.5 0.0 all-reduce.2.cloned.1.call-start
  6.5 0.0 copy-start
  6.5 2.3 %copy.102 = bf16[16,8,24,128]{3,2,1,0:T(8,128)(2,1)} copy(bf16[16,8,24,128]{3,1,2,0:T(8,128)(2,1)} %bitcast.101) | data formatting | bytes 1572864
  8.8 0.0 copy-done.3
  8.8 1.0 copy.103
  9.9 0.0 copy-done
  9.9 1.0 reshape.193
  10.8 1.9 reduce_sum.47
  12.8 11.5 %all-gather = bf16[128,3072]{1,0:T(8,128)(2,1)S(1)} all-gather(bf16[64,3072]{1,0:T(8,128)(2,1)S(1)} %multiply_convert_fusion), channel_id=2, replica_groups=mesh['frame'=16,'row'=2] {'row'}, dimensions={0}, use_global_device_ids=true | all-gather | bytes 1179648 | tf_op jit(solution)/shard_map/all_gather | solution.py:23
  24.3 0.4 copy.70
  24.7 1.5 fusion.45
  26.2 6.0 %pmax.7 = f32[24,128]{1,0:T(8,128)S(1)} all-reduce(f32[24,128]{1,0:T(8,128)S(1)} %get-tuple-element.8), channel_id=1, replica_groups=mesh['frame'=16,'row'=2] {'row'}, use_global_device_ids=true, to_apply=%region_2.0 | all-reduce | flops 3072 | bytes 24576 | tf_op jit(solution)/shard_map/pmax | solution.py:32
  32.2 2.8 %convolution_bitcast_fusion.1 = f32[1,24,128,128]{3,2,1,0:T(8,128)} fusion(f32[24,128,128]{1,2,0:T(8,128)S(1)} %get-tuple-element.9, bf16[128,24,128]{2,1,0:T(8,128)(2,1)} %bitcast.97, f32[24,128]{1,0:T(8,128)S(1)} %pmax.7), kind=kOutput, calls=%fused_computation.24 | convolution fusion | flops 101449728 | bytes 3944448 | tf_op jit(solution)/shard_map/fhat,fthd->fhad/dot_general | solution.py:35
  34.9 0.0 all-reduce.2.cloned.1.call-update
  35.0 0.0 all-gather.4.cloned.1.call-start
  35.0 1.0 copy.104
  36.0 0.0 copy-start.1
  36.1 0.3 fusion.17
  36.3 5.1 %psum.15 = f32[24,128]{1,0:T(8,128)S(1)} all-reduce(f32[24,128]{1,0:T(8,128)S(1)} %fusion.17), channel_id=1, replica_groups=mesh['frame'=16,'row'=2] {'row'}, use_global_device_ids=true, to_apply=%region_5.0 | all-reduce | flops 3072 | bytes 24576 | tf_op jit(solution)/shard_map/psum | solution.py:41
  41.5 0.0 copy-done.1
  41.5 1.1 fusion.42
  42.5 0.4 convolution_multiply_fusion
  42.9 46.9 %all-reduce.2.cloned.1.call-done = f32[1,24,128,128]{3,2,1,0:T(8,128)} async-done(((f32[1,24,128,128]{3,2,1,0:T(8,128)}), f32[1,24,128,128]{3,2,1,0:T(8,128)}) %all-reduce.2.cloned.1.call-update) | async-done | bytes 1572880 | tf_op jit(solution)/shard_map/psum | solution.py:41
  89.8 9.1 %multiply_reduce_fusion = (f32[128]{0:T(128)S(1)}, f32[1,128,24,128]{1,3,2,0:T(8,128)}) fusion(f32[24,128]{1,0:T(8,128)S(1)} %fusion.42, f32[24,128,128]{1,2,0:T(8,128)S(1)} %convolution_multiply_fusion, f32[1,24,128,128]{3,2,1,0:T(8,128)} %all-reduce.2.cloned.1.call-done, f32[24,128]{1,0:T(8,128)S(1)} %psum.15), kind=kOutput, calls=%fused_computation.14 | convolution fusion | flops 103418880 | bytes 4743680 | tf_op jit(solution)/shard_map/fhta,fhad->fthd/dot_general | solution.py:48
  98.9 0.1 rsqrt.12
  98.9 0.0 copy-start.4
  98.9 2.0 copy.79
  100.9 0.0 copy-done.4
  100.9 0.4 fusion.21
  101.3 26.9 %all_to_all.36 = bf16[1,16,8,3072]{3,2,0,1:T(8,128)(2,1)} all-to-all(bf16[1,16,8,3072]{3,2,0,1:T(8,128)(2,1)S(1)} %fusion.21), channel_id=1, replica_groups=mesh['frame'=16,'row'=2] {'frame'}, dimensions={1} | all-to-all | bytes 1572864 | tf_op jit(solution)/shard_map/all_to_all | solution.py:60
  128.2 0.0 all-gather.4.cloned.1.call-update
  128.3 24.4 %all-gather.4.cloned.1.call-done = bf16[1,16,16,3072]{3,2,1,0:T(8,128)(2,1)} async-done(((bf16[1,16,8,3072]{3,2,1,0:T(8,128)(2,1)}), bf16[1,16,16,3072]{3,2,1,0:T(8,128)(2,1)}) %all-gather.4.cloned.1.call-update) | async-done | bytes 1572880 | tf_op jit(solution)/shard_map/all_gather | solution.py:64
  152.7 14.4 %fusion.4 = bf16[16,16,3,1536]{3,1,2,0:T(8,128)(2,1)} fusion(bf16[3072,3,1536]{2,0,1:T(8,128)(2,1)} %param.9, bf16[1,16,16,3072]{3,2,1,0:T(8,128)(2,1)} %all-gather.4.cloned.1.call-done), kind=kOutput, calls=%fused_computation.4 | convolution fusion | flops 7248936960 | bytes 32243712 | tf_op jit(solution)/shard_map/ftd,dcn->ftcn/dot_general | solution.py:62
  167.1 4.2 %reshape.188 = bf16[16,16,3,12,128]{4,3,1,2,0:T(8,128)(2,1)S(1)} reshape(bf16[16,16,3,1536]{3,1,2,0:T(8,128)(2,1)} %fusion.4) | data formatting | bytes 4718592 | tf_op jit(solution)/shard_map/reshape | solution.py:68
  171.3 1.9 fusion.41
  173.1 0.0 copy-start.2
  173.1 3.1 %fusion.48 = (f32[16,12,16]{2,1,0:T(8,128)S(1)}, f32[16,12,16,16]{2,3,1,0:T(8,128)S(1)}) fusion(bf16[16,16,1,12,128]{4,3,1,2,0:T(8,128)(2,1)} %get-tuple-element.7, bf16[16,16,1,12,128]{4,3,1,2,0:T(8,128)(2,1)} %get-tuple-element.6), kind=kOutput, calls=%fused_computation.49 | convolution fusion | flops 12730383 | bytes 1781760 | tf_op jit(solution)/shard_map/sub | solution.py:75
  176.2 0.0 copy-done.2
  176.2 0.7 fusion.19
  176.9 0.3 copy.87
  177.2 0.5 reshape.189
  177.7 0.1 copy.88
  177.8 12.5 %all_to_all.37 = bf16[16,2,1,8,1536]{4,3,0,2,1:T(8,128)(2,1)S(1)} all-to-all(bf16[16,2,1,8,1536]{4,3,0,2,1:T(8,128)(2,1)S(1)} %copy.88), channel_id=1, replica_groups=mesh['frame'=16,'row'=2] {'row'}, dimensions={1} | all-to-all | bytes 1572864 | tf_op jit(solution)/shard_map/all_to_all | solution.py:82
  190.3 0.1 copy.101
  190.4 27.6 %all_to_all.38 = bf16[16,1,1,8,3072]{4,3,2,1,0:T(8,128)(2,1)S(1)} all-to-all(bf16[16,1,1,8,3072]{4,3,2,1,0:T(8,128)(2,1)S(1)} %bitcast.94), channel_id=1, replica_groups=mesh['frame'=16,'row'=2] {'frame'}, dimensions={0} | all-to-all | bytes 1572864 | tf_op jit(solution)/shard_map/all_to_all | solution.py:83
  218.0 0.9 copy.146
  (2 shorter events, 0.1 us)
Async XLA Ops:
  6.5 2.3 %copy-start.3 = (bf16[1,128,3072]{2,1,0:T(8,128)(2,1)S(1)}, bf16[1,128,3072]{2,1,0:T(8,128)(2,1)}, u32[]{:S(2)}) copy-start(bf16[1,128,3072]{2,1,0:T(8,128)(2,1)} %param.7) | copy-start | bytes 2359300
  6.5 83.2 %all-reduce.2.cloned.1.call-start = ((), (), s32[]{:S(2)}) async-start(), calls=%async_computation.3 | async-start | bytes 3145728 | tf_op jit(solution)/shard_map/psum | solution.py:41
  6.5 3.3 %copy-start = (bf16[1,128,3072]{2,1,0:T(8,128)(2,1)S(1)}, bf16[1,128,3072]{2,1,0:T(8,128)(2,1)}, u32[]{:S(2)}) copy-start(bf16[1,128,3072]{2,1,0:T(8,128)(2,1)} %param.5) | copy-start | bytes 2359300
  35.0 117.7 %all-gather.4.cloned.1.call-start = ((), (), s32[]{:S(2)}) async-start(), calls=%async_computation.4 | async-start | bytes 2359296 | tf_op jit(solution)/shard_map/all_gather | solution.py:64
  36.0 5.4 %copy-start.1 = (bf16[16,8,24,128]{3,2,1,0:T(8,128)(2,1)S(1)}, bf16[16,8,24,128]{3,2,1,0:T(8,128)(2,1)}, u32[]{:S(2)}) copy-start(bf16[16,8,24,128]{3,2,1,0:T(8,128)(2,1)} %copy.104) | copy-start | bytes 2359300
  98.9 2.0 copy-start.4
  173.1 3.1 %copy-start.2 = (bf16[16,16,1,12,128]{4,3,1,2,0:T(8,128)(2,1)S(1)}, bf16[16,16,1,12,128]{4,3,1,2,0:T(8,128)(2,1)}, u32[]{:S(2)}) copy-start(bf16[16,16,1,12,128]{4,3,1,2,0:T(8,128)(2,1)} %get-tuple-element.5) | copy-start | bytes 2359300
Sparse Core Ops, SparseCore 0:
  35.1 54.6 all-reduce.1
  128.4 24.2 all-gather.3
where the time goes:
time: 226 us
  blocking collectives  89.7 us (40%)
  waiting for transfers between devices  71.3 us (32%)
  matrix products  32.9 us (15%)
  local copies, waits for them, and re-layouts  15.6 us (7%)
  between operations  13.5 us (6%)
  other arithmetic  2.59 us (1%)
    psum x1, waiting for transfers between devices, local(): agent_totals, agent_numer = lax.psum((agent_totals, agent_numer), 'row')  46.9 us
    all_to_all x1, blocking collectives, local(): lax.all_to_all(gathered_heads, 'frame', split_axis=0, concat_axis=2, tile...  27.6 us
    all_to_all x1, blocking collectives, local(): lax.all_to_all(packed, 'frame', split_axis=1, concat_axis=0, tiled=True)  26.9 us
    all_gather x1, waiting for transfers between devices, local(): lax.all_gather(moved, 'row', axis=1, tiled=True)  24.4 us
    dot_general x1, matrix products, local(): jnp.einsum('ftd,dcn->ftcn', lax.all_gather(moved, 'row', axis=1, tiled=Tr...  14.4 us
    all_to_all x1, blocking collectives, local(): lax.all_to_all(attended, 'row', split_axis=1, concat_axis=4, tiled=True)  12.5 us
    all_gather x1, blocking collectives, local(): lax.all_gather(pooled.astype(jnp.bfloat16), 'row', axis=1, tiled=True)  11.5 us
    dot_general x1, matrix products, local(): jnp.einsum('fhta,fhad->fthd', token_weights, agent_values, preferred_elem...  9.07 us
  transfers between devices with their start and end apart: 2, of which 2 were waited for; matrix products, arithmetic and copies ran while one was open for 1% of the time, Pallas kernels for 0%

commit v1 on v0

--- a/solution.py
+++ b/solution.py
@@ -59,12 +59,22 @@
     packed = normed.reshape(local_frames, frame_count, slot_size, width)
     moved = lax.all_to_all(packed, "frame", split_axis=1, concat_axis=0, tiled=True)
     moved = moved.reshape(all_frames, slot_size, width)
-    projected = jnp.einsum(
-        "ftd,dcn->ftcn",
-        lax.all_gather(moved, "row", axis=1, tiled=True),
-        temporal_weight,
-        preferred_element_type=jnp.float32,
-    )
+    size, place, rows = (lax.axis_size("row"), lax.axis_index("row"), moved.shape[1])
+    upward = [(i, (i + 1) % size) for i in range(size)]
+    current, projected = (moved, None)
+    for step in range(size):
+        holder = (place - step) % size
+        coming = lax.ppermute(current, "row", upward) if step < size - 1 else None
+        made = jnp.einsum(
+            "ftd,dcn->ftcn", current, temporal_weight, preferred_element_type=jnp.float32
+        )
+        length = made.shape[1]
+        if projected is None:
+            projected = jnp.zeros(
+                (*made.shape[:1], size * length, *made.shape[1 + 1 :]), made.dtype
+            )
+        projected = lax.dynamic_update_slice_in_dim(projected, made, holder * length, axis=1)
+        current = coming
     qkv = projected.astype(jnp.bfloat16).reshape(all_frames, locations, 3, group_heads, head_size)
     temporal_scores = (
         jnp.einsum(

time: 226 us -> 213 us (0.942)
  blocking collectives: 89.7 us -> 62.8 us
  matrix products: 32.9 us -> 43.1 us
  starting transfers between devices: 0.04 us -> 6.65 us
  waiting for transfers between devices: 71.3 us -> 67.4 us
    all_to_all x1 -> x0, blocking collectives: 26.9 us -> none  [local(): lax.all_to_all(packed, 'frame', split_axis=1, concat_axis=0, tiled=True)]
    all_gather x1 -> x0, waiting for transfers between devices: 24.4 us -> none  [local(): lax.all_gather(moved, 'row', axis=1, tiled=True)]
    all_to_all x0 -> x1, waiting for transfers between devices: none -> 18.6 us  [local(): lax.all_to_all(packed, 'frame', split_axis=1, concat_axis=0, tiled=True)]
    dot_general x1 -> x2, matrix products: 14.4 us -> 28 us  [local(): jnp.einsum('ftd,dcn->ftcn', current, temporal_weight, preferred_element_t...]
    all_to_all x0 -> x1, starting transfers between devices: none -> 6.37 us  [local(): lax.all_to_all(packed, 'frame', split_axis=1, concat_axis=0, tiled=True)]
    ppermute x0 -> x1, waiting for transfers between devices: none -> 3 us  [local(): coming = lax.ppermute(current, 'row', upward) if step < size - 1 else None]
    unnamed x14 -> x16, local copies, waits for them, and re-layouts: 5.24 us -> 3.4 us
  transfers between devices with their start and end apart: 2 -> 3, of which waited for: 2 -> 3; matrix products, arithmetic and copies ran while one was open for 1% -> 9% of each run, Pallas kernels for 0% -> 0%
where the time goes in v1:
time: 213 us; the launch traced here: 212 us
  waiting for transfers between devices  67.4 us (32%)
  blocking collectives  62.8 us (29%)
  matrix products  43.1 us (20%)
  local copies, waits for them, and re-layouts  15.4 us (7%)
  between operations  13.6 us (6%)
  starting transfers between devices  6.65 us (3%)
  other arithmetic  3.46 us (2%)
    psum x1, waiting for transfers between devices, local(): agent_totals, agent_numer = lax.psum((agent_totals, agent_numer), 'row')  45.8 us
    dot_general x2, matrix products, local(): jnp.einsum('ftd,dcn->ftcn', current, temporal_weight, preferred_element_t...  28 us
    all_to_all x1, blocking collectives, local(): lax.all_to_all(gathered_heads, 'frame', split_axis=0, concat_axis=2, tile...  27.7 us
    all_to_all x1, waiting for transfers between devices, local(): lax.all_to_all(packed, 'frame', split_axis=1, concat_axis=0, tiled=True)  18.6 us
    all_to_all x1, blocking collectives, local(): lax.all_to_all(attended, 'row', split_axis=1, concat_axis=4, tiled=True)  12.3 us
    all_gather x1, blocking collectives, local(): lax.all_gather(pooled.astype(jnp.bfloat16), 'row', axis=1, tiled=True)  11.7 us
    dot_general x1, matrix products, local(): jnp.einsum('fhta,fhad->fthd', token_weights, agent_values, preferred_elem...  7.95 us
    all_to_all x1, starting transfers between devices, local(): lax.all_to_all(packed, 'frame', split_axis=1, concat_axis=0, tiled=True)  6.37 us
  transfers between devices with their start and end apart: 3, of which 3 were waited for; matrix products, arithmetic and copies ran while one was open for 9% of the time, Pallas kernels for 0%

profile of v1, /device:TPU:1, one launch (start us, length us, event | category | flops | bytes accessed | tf_op | source)
XLA Modules:
  0.0 212.4 jit_solution(316546721894746054)
XLA Ops:
  6.5 0.0 all-reduce.2.cloned.1.call-start
  6.5 2.2 %reshape.193 = f32[64,2,3072]{2,1,0:T(2,128)S(1)} reshape(bf16[1,128,3072]{2,1,0:T(8,128)(2,1)} %param.5) | data formatting | bytes 2359296 | tf_op jit(solution)/shard_map/convert_element_type | solution.py:20
  8.7 1.9 reduce_sum.47
  10.6 0.0 copy-start.3
  10.6 11.7 %all-gather = bf16[128,3072]{1,0:T(8,128)(2,1)S(1)} all-gather(bf16[64,3072]{1,0:T(8,128)(2,1)S(1)} %multiply_convert_fusion), channel_id=2, replica_groups=mesh['frame'=16,'row'=2] {'row'}, dimensions={0}, use_global_device_ids=true | all-gather | bytes 1179648 | tf_op jit(solution)/shard_map/all_gather | solution.py:23
  22.3 0.4 copy.65
  22.7 0.0 copy-done.3
  22.7 0.2 copy.97
  22.8 0.0 copy-start.4
  22.9 0.4 fusion.51
  23.2 6.0 %pmax.7 = f32[24,128]{1,0:T(8,128)S(1)} all-reduce(f32[24,128]{1,0:T(8,128)S(1)} %get-tuple-element.8), channel_id=1, replica_groups=mesh['frame'=16,'row'=2] {'row'}, use_global_device_ids=true, to_apply=%region_2.0 | all-reduce | flops 3072 | bytes 24576 | tf_op jit(solution)/shard_map/pmax | solution.py:32
  29.2 0.0 copy-done.4
  29.2 0.2 copy.98
  29.4 1.6 convolution_bitcast_fusion.1
  31.0 0.0 copy-start
  31.0 0.0 all-reduce.2.cloned.1.call-update
  31.1 1.1 copy-done
  32.2 1.0 copy.99
  33.2 0.3 fusion.21
  33.5 5.1 %psum.15 = f32[24,128]{1,0:T(8,128)S(1)} all-reduce(f32[24,128]{1,0:T(8,128)S(1)} %fusion.21), channel_id=1, replica_groups=mesh['frame'=16,'row'=2] {'row'}, use_global_device_ids=true, to_apply=%region_5.0 | all-reduce | flops 3072 | bytes 24576 | tf_op jit(solution)/shard_map/psum | solution.py:41
  38.6 0.0 copy-done.1
  38.6 1.1 fusion.48
  39.7 0.4 convolution_multiply_fusion
  40.1 45.8 %all-reduce.2.cloned.1.call-done = f32[1,24,128,128]{3,2,1,0:T(8,128)} async-done(((f32[1,24,128,128]{3,2,1,0:T(8,128)}), f32[1,24,128,128]{3,2,1,0:T(8,128)}) %all-reduce.2.cloned.1.call-update) | async-done | bytes 1572880 | tf_op jit(solution)/shard_map/psum | solution.py:41
  85.9 7.9 %multiply_reduce_fusion = (f32[128]{0:T(128)S(1)}, f32[1,128,24,128]{1,3,2,0:T(8,128)S(1)}) fusion(f32[24,128]{1,0:T(8,128)S(1)} %fusion.48, f32[24,128,128]{1,2,0:T(8,128)S(1)} %convolution_multiply_fusion, f32[1,24,128,128]{3,2,1,0:T(8,128)} %all-reduce.2.cloned.1.call-done, f32[24,128]{1,0:T(8,128)S(1)} %psum.15), kind=kOutput, calls=%fused_computation.16 | convolution fusion | flops 103418880 | bytes 4743680 | tf_op jit(solution)/shard_map/fhta,fhad->fthd/dot_general | solution.py:48
  93.8 0.6 copy.74
  94.4 0.1 rsqrt.12
  94.5 0.0 copy-done.5
  94.5 1.3 fusion.25
  95.8 6.4 %all-to-all-start = ((bf16[1,16,8,3072]{3,2,0,1:T(8,128)(2,1)}), bf16[1,16,8,3072]{3,2,0,1:T(8,128)(2,1)S(1)}, u32[]{:S(2)}, u32[]{:S(2)}) async-start(bf16[1,16,8,3072]{3,2,0,1:T(8,128)(2,1)} %fusion.25), calls=%async_computation | async-start | bytes 1572864 | tf_op jit(solution)/shard_map/all_to_all | solution.py:60
  102.2 18.6 %all-to-all-done = bf16[1,16,8,3072]{3,2,0,1:T(8,128)(2,1)S(1)} async-done(((bf16[1,16,8,3072]{3,2,0,1:T(8,128)(2,1)}), bf16[1,16,8,3072]{3,2,0,1:T(8,128)(2,1)S(1)}, u32[]{:S(2)}, u32[]{:S(2)}) %all-to-all-start) | async-done | bytes 786464 | tf_op jit(solution)/shard_map/all_to_all | solution.py:60
  120.8 0.3 collective-permute-start
  121.1 1.7 broadcast_in_dim.2
  122.8 14.0 %fusion.6 = bf16[16,16,3,1536]{3,1,2,0:T(8,128)(2,1)} fusion(bf16[16,16,3,1536]{3,1,2,0:T(8,128)(2,1)} %broadcast_in_dim.2, s32[]{:T(128)S(6)} %select_n.18, bf16[3072,3,1536]{2,0,1:T(8,128)(2,1)} %param.9, bf16[1,16,8,3072]{3,2,0,1:T(8,128)(2,1)S(1)} %all-to-all-done), kind=kOutput, calls=%fused_computation.6 | convolution fusion | flops 3623878656 | bytes 31457284 | tf_op jit(solution)/shard_map/ftd,dcn->ftcn/dot_general | solution.py:68
  136.7 3.0 %collective-permute-done = bf16[16,8,3072]{2,1,0:T(8,128)(2,1)S(1)} collective-permute-done((bf16[16,8,3072]{2,1,0:T(8,128)(2,1)S(1)}, bf16[16,8,3072]{2,1,0:T(8,128)(2,1)S(1)}, u32[]{:S(2)}, u32[]{:S(2)}) %collective-permute-start) | collective-permute-done | bytes 786464 | tf_op jit(solution)/shard_map/ppermute | solution.py:67
  139.7 14.0 %fusion.9 = bf16[16,16,3,1536]{3,1,2,0:T(8,128)(2,1)} fusion(bf16[16,16,3,1536]{3,1,2,0:T(8,128)(2,1)} %fusion.6, s32[]{:T(128)S(6)} %select_n.20, bf16[3072,3,1536]{2,0,1:T(8,128)(2,1)} %param.9, bf16[16,8,3072]{2,1,0:T(8,128)(2,1)S(1)} %collective-permute-done), kind=kOutput, calls=%fused_computation.7 | convolution fusion | flops 3623878656 | bytes 31457284 | tf_op jit(solution)/shard_map/ftd,dcn->ftcn/dot_general | solution.py:68
  153.7 4.4 %reshape.188 = bf16[16,16,3,12,128]{4,3,1,2,0:T(8,128)(2,1)S(1)} reshape(bf16[16,16,3,1536]{3,1,2,0:T(8,128)(2,1)} %fusion.9) | data formatting | bytes 4718592 | tf_op jit(solution)/shard_map/reshape | solution.py:78
  158.1 1.9 fusion.47
  160.0 3.1 %fusion.54 = (f32[16,12,16]{2,1,0:T(8,128)S(1)}, f32[16,12,16,16]{2,3,1,0:T(8,128)S(1)}) fusion(bf16[16,16,1,12,128]{4,3,1,2,0:T(8,128)(2,1)} %get-tuple-element.7, bf16[16,16,1,12,128]{4,3,1,2,0:T(8,128)(2,1)} %get-tuple-element.6), kind=kOutput, calls=%fused_computation.53 | convolution fusion | flops 12730383 | bytes 1781760 | tf_op jit(solution)/shard_map/sub | solution.py:85
  163.1 0.0 copy-done.2
  163.1 0.7 fusion.23
  163.8 0.3 copy.81
  164.1 0.5 reshape.189
  164.6 0.1 copy.82
  164.6 12.3 %all_to_all.36 = bf16[16,2,1,8,1536]{4,3,0,2,1:T(8,128)(2,1)S(1)} all-to-all(bf16[16,2,1,8,1536]{4,3,0,2,1:T(8,128)(2,1)S(1)} %copy.82), channel_id=1, replica_groups=mesh['frame'=16,'row'=2] {'row'}, dimensions={1} | all-to-all | bytes 1572864 | tf_op jit(solution)/shard_map/all_to_all | solution.py:92
  176.9 0.1 copy.96
  177.0 27.7 %all_to_all.37 = bf16[16,1,1,8,3072]{4,3,2,1,0:T(8,128)(2,1)S(1)} all-to-all(bf16[16,1,1,8,3072]{4,3,2,1,0:T(8,128)(2,1)S(1)} %bitcast.102), channel_id=1, replica_groups=mesh['frame'=16,'row'=2] {'frame'}, dimensions={0} | all-to-all | bytes 1572864 | tf_op jit(solution)/shard_map/all_to_all | solution.py:93
  204.7 0.9 copy.143
  (5 shorter events, 0.1 us)
Async XLA Ops:
  6.5 79.3 %all-reduce.2.cloned.1.call-start = ((), (), s32[]{:S(2)}) async-start(), calls=%async_computation.3 | async-start | bytes 3145728 | tf_op jit(solution)/shard_map/psum | solution.py:41
  10.6 12.0 %copy-start.3 = (bf16[1,128,3072]{2,1,0:T(8,128)(2,1)S(1)}, bf16[1,128,3072]{2,1,0:T(8,128)(2,1)}, u32[]{:S(2)}) copy-start(bf16[1,128,3072]{2,1,0:T(8,128)(2,1)} %param.6) | copy-start | bytes 2359300
  22.8 6.4 %copy-start.4 = (bf16[1,128,3072]{2,1,0:T(8,128)(2,1)S(1)}, bf16[1,128,3072]{2,1,0:T(8,128)(2,1)}, u32[]{:S(2)}) copy-start(bf16[1,128,3072]{2,1,0:T(8,128)(2,1)} %param.7) | copy-start | bytes 2359300
  31.0 1.1 copy-start
  33.2 5.4 %copy-start.1 = (bf16[16,8,24,128]{3,2,1,0:T(8,128)(2,1)S(1)}, bf16[16,8,24,128]{3,2,1,0:T(8,128)(2,1)}, u32[]{:S(2)}) copy-start(bf16[16,8,24,128]{3,2,1,0:T(8,128)(2,1)} %copy.99) | copy-start | bytes 2359300
  93.8 0.7 copy-start.5
  95.8 25.0 %all-to-all-start = ((bf16[1,16,8,3072]{3,2,0,1:T(8,128)(2,1)}), bf16[1,16,8,3072]{3,2,0,1:T(8,128)(2,1)S(1)}, u32[]{:S(2)}, u32[]{:S(2)}) async-start(bf16[1,16,8,3072]{3,2,0,1:T(8,128)(2,1)} %fusion.25), calls=%async_computation | async-start | bytes 1572864 | tf_op jit(solution)/shard_map/all_to_all | solution.py:60
  120.8 18.9 %collective-permute-start = (bf16[16,8,3072]{2,1,0:T(8,128)(2,1)S(1)}, bf16[16,8,3072]{2,1,0:T(8,128)(2,1)S(1)}, u32[]{:S(2)}, u32[]{:S(2)}) collective-permute-start(bf16[16,8,3072]{2,1,0:T(8,128)(2,1)S(1)} %bitcast.100), channel_id=1, source_target_pairs={{0,1},{1,0},{2,3},{3,2},{4,5},{5,4},{6,7},{7,6},{8,9},{9,8},{10,11... | collective-permute-start | bytes 2359304 | tf_op jit(solution)/shard_map/ppermute | solution.py:67
  160.0 3.1 %copy-start.2 = (bf16[16,16,1,12,128]{4,3,1,2,0:T(8,128)(2,1)S(1)}, bf16[16,16,1,12,128]{4,3,1,2,0:T(8,128)(2,1)}, u32[]{:S(2)}) copy-start(bf16[16,16,1,12,128]{4,3,1,2,0:T(8,128)(2,1)} %get-tuple-element.5) | copy-start | bytes 2359300
Sparse Core Ops, SparseCore 0:
  31.2 54.6 all-reduce.1
